TPU v7x, 32 devices: a whole 2x2x4 slice. The times are simulated.
32 devices in a mesh: grp: 8 (over z, core), row: 4 (over y, x).
Axes of the slice: x: 2, y: 2, z: 4, core: 2. Of those that a mesh axis runs over, the one named last changes fastest.
Arguments:
- theta: float32 [16, 512, 512], P('grp', 'row'), may hold values from -8 to 8
- left_env: bfloat16 [16, 8, 512, 512], P('grp', None, 'row'), may hold values from -1.5 to 1.5
- right_env: bfloat16 [16, 8, 512, 512], P('grp', None, 'row'), may hold values from -3.5 to 3.5
- lengths: int32 [16, 2], P('grp'), may hold values from 128 to 512
Outputs:
- evolved: float32 [16, 512, 512], P('grp', 'row')
- hessenberg: float32 [8, 8], replicated
All inputs are finite; a program needn't handle non-finite values.
Results may differ from a plain program's by a relative error of at most 0.0029.
Values may be sent and summed in bfloat16 or wider, within the bound.
A program may use at most 64 MiB of HBM per device.

v0:
```python
import jax
import jax.numpy as jnp
from jax import lax
from jax.sharding import PartitionSpec as P

KRYLOV = 8


epsilon = 1e-06
time_step = 0.5


def propagate(hessenberg):
    krylov_size = hessenberg.shape[0]
    scaled = time_step * hessenberg
    series = jnp.eye(krylov_size, dtype=jnp.float32)
    series_term = jnp.eye(krylov_size, dtype=jnp.float32)
    for degree in range(1, 19):
        series_term = jnp.dot(series_term, scaled, precision=lax.Precision.HIGHEST) / degree
        series = series + series_term
    return series[:, 0]


def local(theta, left_env, right_env, lengths):
    local_rows = theta.shape[1]
    sect_width = theta.shape[2]
    row_start = lax.axis_index("row") * local_rows
    row_ids = row_start + lax.broadcasted_iota(jnp.int32, (1, local_rows, 1), 1)
    col_ids = lax.broadcasted_iota(jnp.int32, (1, 1, sect_width), 2)
    live_mask = (
        (row_ids < lengths[:, 0][:, None, None]) & (col_ids < lengths[:, 1][:, None, None])
    ).astype(jnp.float32)
    right_full = lax.all_gather(right_env, "row", axis=2, tiled=True)
    start_block = theta * live_mask
    norm_zero = jnp.sqrt(lax.psum(jnp.sum(start_block * start_block), ("grp", "row")) + epsilon)
    krylov_basis = [start_block / norm_zero]
    krylov_size = KRYLOV
    hessenberg = jnp.zeros((krylov_size, krylov_size), jnp.float32)
    for column in range(krylov_size):
        packed = krylov_basis[column].astype(jnp.bfloat16)
        inner_terms = jnp.einsum(
            "sab,swbc->swac", packed, right_full, preferred_element_type=jnp.float32
        )
        inner_terms = inner_terms.astype(jnp.bfloat16)
        partial_image = jnp.einsum(
            "swba,swbc->sac", left_env, inner_terms, preferred_element_type=jnp.float32
        )
        image = lax.psum_scatter(partial_image, "row", scatter_dimension=1, tiled=True) * live_mask
        local_dots = jnp.stack([jnp.sum(vector * image) for vector in krylov_basis])
        coefficients, squared = lax.psum((local_dots, jnp.sum(image * image)), ("grp", "row"))
        for previous in range(column + 1):
            image = image - coefficients[previous] * krylov_basis[previous]
        hessenberg = hessenberg.at[: column + 1, column].set(coefficients)
        if column + 1 < krylov_size:
            beta_norm = jnp.sqrt(squared - jnp.sum(coefficients * coefficients) + epsilon)
            hessenberg = hessenberg.at[column + 1, column].set(beta_norm)
            krylov_basis.append(image / beta_norm)
    weights = propagate(hessenberg)
    evolved = jnp.zeros_like(start_block)
    for column in range(krylov_size):
        evolved = evolved + weights[column] * krylov_basis[column]
    return (norm_zero * evolved, hessenberg)


def solution(mesh):
    return jax.shard_map(
        local,
        mesh=mesh,
        in_specs=(
            P("grp", "row", None),
            P("grp", None, "row", None),
            P("grp", None, "row", None),
            P("grp", None),
        ),
        out_specs=(P("grp", "row", None), P()),
        check_vma=False,
    )
```

profile of v0, /device:TPU:1, one launch (start us, length us, event | category | flops | bytes accessed | tf_op | source)
XLA Modules:
  0.0 889.9 jit_solution(13568998900987345164)
XLA Ops:
  9.7 41.5 %psum.112 = f32[]{:T(128)} all-reduce(f32[]{:T(128)} %multiply_reduce_fusion.43), channel_id=1, replica_groups=mesh['grp'=8,'row'=4] {'grp','row'}, use_global_device_ids=true, to_apply=%region_1.0 | all-reduce | flops 1 | bytes 8 | tf_op jit(solution)/shard_map/psum | solution.py:35
  51.9 47.6 %all-gather.2.cloned.1.call-done = bf16[2,8,512,512]{3,2,1,0:T(8,128)(2,1)} async-done(((bf16[2,8,128,512]{3,2,1,0:T(8,128)(2,1)}), bf16[2,8,512,512]{3,2,1,0:T(8,128)(2,1)}) %all-gather.2.cloned.1.call-update) | async-done | bytes 8388624 | tf_op jit(solution)/shard_map/all_gather | solution.py:33
  99.5 8.9 fusion.24
  108.5 35.3 %reduce-scatter.9.cloned.1.call-done = f32[2,128,512]{1,2,0:T(8,128)} async-done(((f32[2,512,512]{1,2,0:T(8,128)}), f32[2,128,512]{1,2,0:T(8,128)}) %reduce-scatter.9.cloned.1.call-update) | async-done | bytes 524304 | tf_op jit(solution)/shard_map/reduce_scatter | solution.py:48
  145.7 39.1 %all-reduce.7 = (f32[]{:T(128)}, f32[1]{0:T(128)}) all-reduce(f32[]{:T(128)} %get-tuple-element.226, f32[1]{0:T(128)} %bitcast.6), channel_id=1, replica_groups=mesh['grp'=8,'row'=4] {'grp','row'}, use_global_device_ids=true, to_apply=%region_6.0 | all-reduce | flops 2 | bytes 16 | tf_op jit(solution)/shard_map/psum | solution.py:50
  197.4 36.7 %reduce-scatter.11.cloned.1.call-done = f32[2,128,512]{1,2,0:T(8,128)} async-done(((f32[2,512,512]{1,2,0:T(8,128)}), f32[2,128,512]{1,2,0:T(8,128)}) %reduce-scatter.11.cloned.1.call-update) | async-done | bytes 524304 | tf_op jit(solution)/shard_map/reduce_scatter | solution.py:48
  237.3 39.3 %all-reduce.6 = (f32[]{:T(128)}, f32[2]{0:T(128)S(1)}) all-reduce(f32[]{:T(128)} %get-tuple-element.224, f32[2]{0:T(128)S(1)} %pad_maximum_fusion), channel_id=1, replica_groups=mesh['grp'=8,'row'=4] {'grp','row'}, use_global_device_ids=true, to_apply=%region_12.0 | all-reduce | flops 3 | bytes 24 | tf_op jit(solution)/shard_map/psum | solution.py:50
  282.3 8.9 fusion.34
  291.2 36.7 %reduce-scatter.13.cloned.1.call-done = f32[2,128,512]{1,2,0:T(8,128)} async-done(((f32[2,512,512]{1,2,0:T(8,128)}), f32[2,128,512]{1,2,0:T(8,128)}) %reduce-scatter.13.cloned.1.call-update) | async-done | bytes 524304 | tf_op jit(solution)/shard_map/reduce_scatter | solution.py:48
  332.1 39.1 %all-reduce.5 = (f32[]{:T(128)}, f32[3]{0:T(128)S(1)}) all-reduce(f32[]{:T(128)} %get-tuple-element.221, f32[3]{0:T(128)S(1)} %pad_maximum_fusion.1), channel_id=1, replica_groups=mesh['grp'=8,'row'=4] {'grp','row'}, use_global_device_ids=true, to_apply=%region_21.0 | all-reduce | flops 4 | bytes 32 | tf_op jit(solution)/shard_map/psum | solution.py:50
  377.8 8.9 fusion.39
  386.7 36.7 %reduce-scatter.15.cloned.1.call-done = f32[2,128,512]{1,2,0:T(8,128)} async-done(((f32[2,512,512]{1,2,0:T(8,128)}), f32[2,128,512]{1,2,0:T(8,128)}) %reduce-scatter.15.cloned.1.call-update) | async-done | bytes 524304 | tf_op jit(solution)/shard_map/reduce_scatter | solution.py:48
  428.3 39.5 %all-reduce.4 = (f32[]{:T(128)}, f32[4]{0:T(128)S(1)}) all-reduce(f32[]{:T(128)} %get-tuple-element.217, f32[4]{0:T(128)S(1)} %pad_maximum_fusion.2), channel_id=1, replica_groups=mesh['grp'=8,'row'=4] {'grp','row'}, use_global_device_ids=true, to_apply=%region_31.0 | all-reduce | flops 5 | bytes 40 | tf_op jit(solution)/shard_map/psum | solution.py:50
  475.4 8.9 fusion.44
  484.3 36.7 %reduce-scatter.17.cloned.1.call-done = f32[2,128,512]{1,2,0:T(8,128)} async-done(((f32[2,512,512]{1,2,0:T(8,128)}), f32[2,128,512]{1,2,0:T(8,128)}) %reduce-scatter.17.cloned.1.call-update) | async-done | bytes 524304 | tf_op jit(solution)/shard_map/reduce_scatter | solution.py:48
  526.7 39.0 %all-reduce.3 = (f32[]{:T(128)}, f32[5]{0:T(128)S(1)}) all-reduce(f32[]{:T(128)} %get-tuple-element.211, f32[5]{0:T(128)S(1)} %stack.147), channel_id=1, replica_groups=mesh['grp'=8,'row'=4] {'grp','row'}, use_global_device_ids=true, to_apply=%region_42.0 | all-reduce | flops 6 | bytes 48 | tf_op jit(solution)/shard_map/psum | solution.py:50
  574.2 8.9 fusion.49
  583.2 36.7 %reduce-scatter.19.cloned.1.call-done = f32[2,128,512]{1,2,0:T(8,128)} async-done(((f32[2,512,512]{1,2,0:T(8,128)}), f32[2,128,512]{1,2,0:T(8,128)}) %reduce-scatter.19.cloned.1.call-update) | async-done | bytes 524304 | tf_op jit(solution)/shard_map/reduce_scatter | solution.py:48
  626.5 39.2 %all-reduce.2 = (f32[]{:T(128)}, f32[6]{0:T(128)S(1)}) all-reduce(f32[]{:T(128)} %get-tuple-element.205, f32[6]{0:T(128)S(1)} %stack.154), channel_id=1, replica_groups=mesh['grp'=8,'row'=4] {'grp','row'}, use_global_device_ids=true, to_apply=%region_54.0 | all-reduce | flops 7 | bytes 56 | tf_op jit(solution)/shard_map/psum | solution.py:50
  675.0 8.9 fusion.54
  683.9 36.7 %reduce-scatter.21.cloned.1.call-done = f32[2,128,512]{1,2,0:T(8,128)} async-done(((f32[2,512,512]{1,2,0:T(8,128)}), f32[2,128,512]{1,2,0:T(8,128)}) %reduce-scatter.21.cloned.1.call-update) | async-done | bytes 524304 | tf_op jit(solution)/shard_map/reduce_scatter | solution.py:48
  728.1 39.0 %all-reduce.1 = (f32[]{:T(128)}, f32[7]{0:T(128)S(1)}) all-reduce(f32[]{:T(128)} %get-tuple-element.198, f32[7]{0:T(128)S(1)} %stack.162), channel_id=1, replica_groups=mesh['grp'=8,'row'=4] {'grp','row'}, use_global_device_ids=true, to_apply=%region_67.0 | all-reduce | flops 8 | bytes 64 | tf_op jit(solution)/shard_map/psum | solution.py:50
  777.0 8.9 fusion.59
  831.1 38.7 %psum.127 = f32[8,1]{1,0:T(8,128)S(1)} all-reduce(f32[8,1]{1,0:T(8,128)S(1)} %copy.13), channel_id=1, replica_groups=mesh['grp'=8,'row'=4] {'grp','row'}, use_global_device_ids=true, to_apply=%region_78.0 | all-reduce | flops 8 | bytes 64 | tf_op jit(solution)/shard_map/psum | solution.py:50
  (143 shorter events, 145.4 us)
Async XLA Ops:
  7.2 92.4 %copy-start = (bf16[2,8,128,512]{3,2,1,0:T(8,128)(2,1)S(1)}, bf16[2,8,128,512]{3,2,1,0:T(8,128)(2,1)}, u32[]{:S(2)}) copy-start(bf16[2,8,128,512]{3,2,1,0:T(8,128)(2,1)} %param.35) | copy-start | bytes 6291460
  7.2 1.2 copy-start.2
  7.2 1.4 copy-start.3
  7.2 92.3 %all-gather.2.cloned.1.call-start = ((), (), s32[]{:S(2)}) async-start(), calls=%async_computation.8 | async-start | bytes 10485760 | tf_op jit(solution)/shard_map/all_gather | solution.py:33
  7.9 135.8 %reduce-scatter.9.cloned.1.call-start = ((), (), s32[]{:S(2)}) async-start(), calls=%async_computation.9 | async-start | bytes 2621440 | tf_op jit(solution)/shard_map/reduce_scatter | solution.py:48
  108.4 125.6 %reduce-scatter.11.cloned.1.call-start = ((), (), s32[]{:S(2)}) async-start(), calls=%async_computation.10 | async-start | bytes 2621440 | tf_op jit(solution)/shard_map/reduce_scatter | solution.py:48
  197.3 130.6 %reduce-scatter.13.cloned.1.call-start = ((), (), s32[]{:S(2)}) async-start(), calls=%async_computation.11 | async-start | bytes 2621440 | tf_op jit(solution)/shard_map/reduce_scatter | solution.py:48
  291.2 132.3 %reduce-scatter.15.cloned.1.call-start = ((), (), s32[]{:S(2)}) async-start(), calls=%async_computation.12 | async-start | bytes 2621440 | tf_op jit(solution)/shard_map/reduce_scatter | solution.py:48
  386.7 134.3 %reduce-scatter.17.cloned.1.call-start = ((), (), s32[]{:S(2)}) async-start(), calls=%async_computation.13 | async-start | bytes 2621440 | tf_op jit(solution)/shard_map/reduce_scatter | solution.py:48
  484.3 135.7 %reduce-scatter.19.cloned.1.call-start = ((), (), s32[]{:S(2)}) async-start(), calls=%async_computation.14 | async-start | bytes 2621440 | tf_op jit(solution)/shard_map/reduce_scatter | solution.py:48
  583.1 137.5 %reduce-scatter.21.cloned.1.call-start = ((), (), s32[]{:S(2)}) async-start(), calls=%async_computation.15 | async-start | bytes 2621440 | tf_op jit(solution)/shard_map/reduce_scatter | solution.py:48
  683.9 138.9 %reduce-scatter.23.cloned.1.call-start = ((), (), s32[]{:S(2)}) async-start(), calls=%async_computation.16 | async-start | bytes 2621440 | tf_op jit(solution)/shard_map/reduce_scatter | solution.py:48
  785.9 3.8 copy-start.8
  785.9 4.5 copy-start.7
  785.9 5.2 copy-start.6
  785.9 5.9 copy-start.5
  785.9 6.6 copy-start.4
  869.9 11.2 %copy-start.1 = (f32[8,8]{1,0:T(8,128)}, f32[8,8]{1,0:T(8,128)S(1)}, u32[]{:S(2)}) copy-start(f32[8,8]{1,0:T(8,128)S(1)} %scatter.74) | copy-start | bytes 772
Sparse Core Ops, SparseCore 0:
  9.9 89.6 all-gather.1
  108.6 35.1 reduce-scatter.8
  197.4 36.5 reduce-scatter.10
  291.3 36.5 reduce-scatter.12
  386.8 36.5 reduce-scatter.14
  484.4 36.5 reduce-scatter.16
  583.3 36.6 reduce-scatter.18
  684.0 36.6 reduce-scatter.20
  786.1 36.6 reduce-scatter.22
where the time goes:
time: 901 us; the launch traced here: 890 us
  blocking collectives  354 us (39%)
  waiting for transfers between devices  313 us (35%)
  other arithmetic  85.4 us (9%)
  matrix products  73.3 us (8%)
  local copies, waits for them, and re-layouts  39 us (4%)
  between operations  24.8 us (3%)
    psum x8, blocking collectives, local(): lax.psum((local_dots, jnp.sum(image * image)), ('grp', 'row'))  313 us
    reduce_scatter x8, waiting for transfers between devices, local(): lax.psum_scatter(partial_image, 'row', scatter_dimension=1, tiled=True)  264 us
    dot_general x8, matrix products, local(): jnp.einsum('swba,swbc->sac', left_env, inner_terms, preferred_element_typ...  70.8 us
    all_gather x1, waiting for transfers between devices, local(): right_full = lax.all_gather(right_env, 'row', axis=2, tiled=True)  47.6 us
    psum x1, blocking collectives, local(): lax.psum(jnp.sum(start_block * start_block), ('grp', 'row')) + epsilon  41.5 us
    div x7, other arithmetic, local(): krylov_basis.append(image / beta_norm)  34 us
    reduce_sum x8, other arithmetic, local(): local_dots = jnp.stack([jnp.sum(vector * image) for vector in krylov_basis])  19.7 us
  transfers between devices with their start and end apart: 9, of which 9 were waited for; matrix products, arithmetic and copies ran while one was open for 3% of the time, Pallas kernels for 0%

commit v1 on v0

v1 whole, which is shorter than its diff:
```python
import functools

import jax
import jax.numpy as jnp
from jax import lax
from jax.experimental import pallas as pl
from jax.experimental.pallas import tpu as pltpu
from jax.sharding import PartitionSpec as P

KRYLOV = 8
DEGREES = 19
ROWS = 64

epsilon = 1e-06
time_step = 0.5
MESH = pl.DeviceIdType.MESH
F32 = jnp.float32
BF16 = jnp.bfloat16


def kernel(ngrp, nrow, lengths, theta, left, right, out, hess,
           masked, meta, l_land, l_t, r_land, q, basis, v, acc, live, msg, slots, h_t, evolved,
           th_send, th_recv, meta_send, meta_recv, l_send, l_recv, f_send, f_recv,
           r_send, r_recv, v_send, v_recv, m_send, m_recv, o_send, o_recv):
    S, lr, width = theta.shape
    W = left.shape[1]
    half = width // 2
    K = KRYLOV
    n = ngrp * nrow
    rep = nrow // (2 * S)
    g, r = lax.axis_index("grp"), lax.axis_index("row")
    me = g * nrow + r
    p = g % 2
    base = g - p
    partner = (base + 1 - p, r)
    owner = r // (S * rep)
    sector = (r // rep) % S
    my_cols = pl.ds(pl.multiple_of(p * half, half), half)
    my_rows = pl.ds(pl.multiple_of(r * lr, lr), lr)

    barrier = pltpu.get_barrier_semaphore()

    def greet(o, c):
        t = (me + o) % n
        pl.semaphore_signal(barrier, inc=1, device_id=(t // nrow, t % nrow), device_id_type=MESH)
        return c

    lax.fori_loop(1, n, greet, 0)

    lane = lax.broadcasted_iota(jnp.int32, (1, 128), 1)
    square = jnp.zeros((8, width), F32)
    for s in range(S):
        for k in range(2):
            meta[p, pl.ds(2 * s + k, 1), :] = jnp.full((1, 128), lengths[s, k].astype(F32))
        row_ids = r * lr + lax.broadcasted_iota(jnp.int32, (lr, width), 0)
        col_ids = lax.broadcasted_iota(jnp.int32, (lr, width), 1)
        keep = (row_ids < lengths[s, 0]) & (col_ids < lengths[s, 1])
        block = jnp.where(keep, theta[s], 0.0)
        masked[s] = block
        square = square + jnp.sum((block * block).reshape(lr // 8, 8, width), axis=0)
    for k in range(1, K):
        basis[k] = jnp.zeros((width, half), F32)
    h_t[...] = jnp.zeros_like(h_t)

    pl.semaphore_wait(barrier, n - 1)

    def put(src, dst, send, recv, dev, own):
        @pl.when(own)
        def _():
            pltpu.make_async_copy(src, dst, recv).start()

        @pl.when(jnp.logical_not(own))
        def _():
            pltpu.make_async_remote_copy(src_ref=src, dst_ref=dst, send_sem=send, recv_sem=recv,
                                         device_id=dev, device_id_type=MESH).start()

    def put_done(src, send, own):
        @pl.when(jnp.logical_not(own))
        def _():
            pltpu.make_async_copy(src, src, send).wait()

    def got(dst, recv):
        pltpu.make_async_copy(dst, dst, recv).wait()

    def share(k, row):
        msg[k] = row
        slots[k, me] = row

        def one(o, c):
            t = (me + o) % n
            pltpu.make_async_remote_copy(src_ref=msg.at[k], dst_ref=slots.at[k, me], send_sem=m_send.at[k],
                                         recv_sem=m_recv.at[k], device_id=(t // nrow, t % nrow),
                                         device_id_type=MESH).start()
            return c

        lax.fori_loop(1, n, one, 0)

    def shared(k):
        rest = slots.at[k, pl.ds(0, n - 1)]
        pltpu.make_async_copy(rest, rest, m_recv.at[k]).wait()
        pltpu.make_async_copy(rest, rest, m_send.at[k]).wait()
        return jnp.sum(slots[k], axis=0)

    def pick(row, i):
        return jnp.sum(jnp.where(lane == i, row, 0.0), axis=1, keepdims=True)

    meta_copy = pltpu.make_async_remote_copy(src_ref=meta.at[p], dst_ref=meta.at[p], send_sem=meta_send,
                                             recv_sem=meta_recv, device_id=partner, device_id_type=MESH)
    meta_copy.start()
    share(K, jnp.where(lane == 0, jnp.sum(square), 0.0))

    targets = [(s, j, (p * S + s) * rep + j) for s in range(S) for j in range(rep)]

    def theta_piece(s, c):
        return masked.at[s, :, pl.ds(c * half, half)]

    for s, j, t in targets:
        for c in range(2):
            put(theta_piece(s, c), basis.at[0, my_rows, :], th_send.at[s, j, c], th_recv.at[r],
                (base + c, t), (t == r) & (p == c))

    def env(w, carry):
        for s, j, t in targets:
            for c in range(2):
                put(right.at[s, w, :, pl.ds(c * half, half)], r_land.at[w, my_rows, :],
                    r_send.at[w, s, j, c], r_recv.at[w, r], (base + c, t), (t == r) & (p == c))
            put(left.at[s, w], l_land.at[w, my_rows, :], l_send.at[w, s, j], l_recv.at[w, r],
                (base + w % 2, t), (t == r) & (p == w % 2))
        return carry

    lax.fori_loop(0, W, env, 0)

    pltpu.make_async_copy(meta.at[1 - p], meta.at[1 - p], meta_recv).wait()
    a_len = meta[owner, pl.ds(2 * sector, 1), :]
    c_len = meta[owner, pl.ds(2 * sector + 1, 1), :]
    a_len = jnp.concatenate([a_len] * (half // 128), axis=1)
    c_len = jnp.concatenate([c_len] * (half // 128), axis=1)
    row_ids = lax.broadcasted_iota(jnp.int32, (width, half), 0).astype(F32)
    col_ids = (p * half + lax.broadcasted_iota(jnp.int32, (width, half), 1)).astype(F32)
    live[...] = jnp.where((row_ids < a_len) & (col_ids < c_len), 1.0, 0.0)

    def v_copy(j):
        return pltpu.make_async_remote_copy(src_ref=v.at[j, :, my_cols], dst_ref=v.at[j, :, my_cols],
                                            send_sem=v_send.at[j], recv_sem=v_recv.at[j],
                                            device_id=partner, device_id_type=MESH)

    norm_zero = jnp.sqrt(pick(shared(K), 0) + epsilon)
    for i in range(nrow):
        got(basis.at[0, pl.ds(i * lr, lr), :], th_recv.at[i])

    def start_chunk(i, c):
        rows = pl.ds(pl.multiple_of(i * ROWS, ROWS), ROWS)
        b = basis[0, rows, :] / norm_zero
        basis[0, rows, :] = b
        v[0, rows, my_cols] = b.astype(BF16)
        return c

    lax.fori_loop(0, width // ROWS, start_chunk, 0)
    first = v_copy(0)
    first.start()
    first.wait()

    def forward_copy(w):
        return pltpu.make_async_remote_copy(src_ref=l_land.at[w], dst_ref=l_land.at[w], send_sem=f_send.at[w],
                                            recv_sem=f_recv.at[w], device_id=partner, device_id_type=MESH)

    def image_zero(pair, carry):
        mine = 2 * pair + p
        for i in range(nrow):
            got(l_land.at[mine, pl.ds(i * lr, lr), :], l_recv.at[mine, i])
        forward_copy(mine).start()
        for step in range(2):
            w = 2 * pair + step
            for i in range(nrow):
                got(r_land.at[w, pl.ds(i * lr, lr), :], r_recv.at[w, i])
            at = pl.ds(pl.multiple_of(w * width, width), width)
            q[at, :] = jnp.dot(v[0], r_land[w], preferred_element_type=F32).astype(BF16)
        theirs = 2 * pair + 1 - p
        got(l_land.at[theirs], f_recv.at[theirs])
        for step in range(2):
            w = 2 * pair + step
            at = pl.ds(pl.multiple_of(w * width, width), width)
            l_t[:, at] = l_land[w].T
        return carry

    lax.fori_loop(0, W // 2, image_zero, 0)

    def outer():
        acc[...] = jnp.dot(l_t[...], q[...], preferred_element_type=F32)

    outer()

    counts = jnp.where(r % rep == 0, 1.0, 0.0)

    def coefficients(j):
        def chunk(i, sums):
            rows = pl.ds(pl.multiple_of(i * ROWS, ROWS), ROWS)
            u = acc[rows, :] * live[rows, :]
            acc[rows, :] = u
            new = []
            for k in range(K + 1):
                other = basis[k, rows, :] if k < K else u
                new.append(sums[k] + jnp.sum((other * u).reshape(ROWS // 8, 8, half), axis=0))
            return tuple(new)

        zero = jnp.zeros((8, half), F32)
        sums = lax.fori_loop(0, width // ROWS, chunk, (zero,) * (K + 1))
        row = jnp.zeros((1, 128), F32)
        for k in range(K + 1):
            row = jnp.where(lane == k, jnp.sum(sums[k]), row)
        share(j, row * counts)
        return shared(j)

    def step(j, carry):
        row = coefficients(j)
        dots = jnp.where(lane < K, row, 0.0)
        left_over = pick(row, K) - jnp.sum(dots * dots, axis=1, keepdims=True)
        beta = jnp.sqrt(jnp.maximum(left_over, 0.0) + epsilon)
        h_t[pl.ds(j, 1), :] = jnp.where(lane == j + 1, beta, dots)
        coef = [pick(row, k) for k in range(K)]
        scale = 1.0 / beta

        def chunk(i, c):
            rows = pl.ds(pl.multiple_of(i * ROWS, ROWS), ROWS)
            u = acc[rows, :]
            for k in range(K):
                u = u - coef[k] * basis[k, rows, :]
            u = u * scale
            basis[j + 1, rows, :] = u
            v[j + 1, rows, my_cols] = u.astype(BF16)
            return c

        lax.fori_loop(0, width // ROWS, chunk, 0)
        copy = v_copy(j + 1)
        copy.start()
        copy.wait()
        vec = v.at[j + 1]

        for w in range(W):
            q[w * width:(w + 1) * width, :] = jnp.dot(vec[...], r_land[w], preferred_element_type=F32).astype(BF16)
        outer()
        return carry

    lax.fori_loop(0, K - 1, step, 0)
    row = coefficients(K - 1)
    h_t[pl.ds(K - 1, 1), :] = jnp.where(lane < K, row, 0.0)

    ht = h_t[...]
    sub = lax.broadcasted_iota(jnp.int32, (K, 128), 0)
    lanes = lax.broadcasted_iota(jnp.int32, (K, 128), 1)
    h = jnp.zeros((K, 128), F32)
    for j in range(K):
        column = jnp.sum(jnp.where(lanes == sub, ht[j:j + 1, :], 0.0), axis=1, keepdims=True)
        h = jnp.where(lanes == j, column, h)
    hess[...] = h[:, :K]
    term = jnp.where(lane == 0, 1.0, 0.0)
    series_row = term
    series_col = jnp.zeros((K, 1), F32)
    for degree in range(1, DEGREES):
        if degree % 2:
            term = jnp.sum((time_step * h) * term, axis=1, keepdims=True) * (1.0 / degree)
            series_col = series_col + term
        else:
            term = jnp.sum((time_step * ht) * term, axis=0, keepdims=True) * (1.0 / degree)
            series_row = series_row + term
    weights = [(pick(series_row, k) + series_col[k:k + 1, :]) * norm_zero for k in range(K)]

    def sum_chunk(i, c):
        rows = pl.ds(pl.multiple_of(i * ROWS, ROWS), ROWS)
        total = weights[0] * basis[0, rows, :]
        for k in range(1, K):
            total = total + weights[k] * basis[k, rows, :]
        evolved[rows, :] = total
        return c

    lax.fori_loop(0, width // ROWS, sum_chunk, 0)

    for t in range(nrow):
        @pl.when(r % rep == t % rep)
        def _():
            put(evolved.at[pl.ds(t * lr, lr), :], out.at[sector, :, my_cols], o_send.at[t],
                o_recv.at[sector, p], (base + owner, t), (r == t) & (p == owner))

    for s in range(S):
        for c in range(2):
            got(out.at[s, :, pl.ds(c * half, half)], o_recv.at[s, c])
    for t in range(nrow):
        @pl.when(r % rep == t % rep)
        def _():
            put_done(evolved.at[pl.ds(t * lr, lr), :], o_send.at[t], (r == t) & (p == owner))
    meta_copy.wait_send()
    for s, j, t in targets:
        for c in range(2):
            put_done(theta_piece(s, c), th_send.at[s, j, c], (t == r) & (p == c))

    def env_done(w, carry):
        for s, j, t in targets:
            for c in range(2):
                put_done(right.at[s, w, :, pl.ds(c * half, half)], r_send.at[w, s, j, c], (t == r) & (p == c))
            put_done(left.at[s, w], l_send.at[w, s, j], (t == r) & (p == w % 2))
        return carry

    lax.fori_loop(0, W, env_done, 0)

    def forward_done(pair, carry):
        forward_copy(2 * pair + p).wait_send()
        return carry

    lax.fori_loop(0, W // 2, forward_done, 0)


def local(ngrp, nrow, theta, left_env, right_env, lengths):
    S, lr, width = theta.shape
    W = left_env.shape[1]
    half = width // 2
    n = ngrp * nrow
    rep = nrow // (2 * S)
    K = KRYLOV
    dma = pltpu.SemaphoreType.DMA
    vmem = pl.BlockSpec(memory_space=pltpu.VMEM)
    hbm = pl.BlockSpec(memory_space=pl.ANY)
    return pl.pallas_call(
        functools.partial(kernel, ngrp, nrow),
        out_shape=(jax.ShapeDtypeStruct(theta.shape, F32), jax.ShapeDtypeStruct((K, K), F32)),
        in_specs=[pl.BlockSpec(memory_space=pltpu.SMEM), vmem, hbm, hbm],
        out_specs=(hbm, vmem),
        scratch_shapes=[
            pltpu.VMEM((S, lr, width), F32),
            pltpu.VMEM((2, 8 * ((2 * S + 7) // 8), 128), F32),
            pltpu.VMEM((W, width, width), BF16),
            pltpu.VMEM((width, W * width), BF16),
            pltpu.VMEM((W, width, half), BF16),
            pltpu.VMEM((W * width, half), BF16),
            pltpu.VMEM((K, width, half), F32),
            pltpu.VMEM((K, width, width), BF16),
            pltpu.VMEM((width, half), F32),
            pltpu.VMEM((width, half), F32),
            pltpu.VMEM((K + 1, 1, 128), F32),
            pltpu.VMEM((K + 1, n, 1, 128), F32),
            pltpu.VMEM((K, 128), F32),
            pltpu.VMEM((width, half), F32),
            dma((S, rep, 2)), dma((nrow,)), dma, dma,
            dma((W, S, rep)), dma((W, nrow)), dma((W,)), dma((W,)),
            dma((W, S, rep, 2)), dma((W, nrow)), dma((K,)), dma((K,)),
            dma((K + 1,)), dma((K + 1,)), dma((nrow,)), dma((S, 2)),
        ],
        compiler_params=pltpu.CompilerParams(collective_id=0, has_side_effects=True,
                                             vmem_limit_bytes=60 * 1024 * 1024),
    )(lengths, theta, left_env, right_env)


def solution(mesh):
    return jax.shard_map(
        functools.partial(local, mesh.shape["grp"], mesh.shape["row"]),
        mesh=mesh,
        in_specs=(
            P("grp", "row", None),
            P("grp", None, "row", None),
            P("grp", None, "row", None),
            P("grp", None),
        ),
        out_specs=(P("grp", "row", None), P()),
        check_vma=False,
    )
```

time: 901 us -> 152 us (0.17); the launches traced: 890 us -> 151 us
  blocking collectives: 354 us -> 0 us
  waiting for transfers between devices: 313 us -> 0 us
  Pallas kernels: 0 us -> 148 us
  other arithmetic: 85.4 us -> 0 us
  matrix products: 73.3 us -> 0 us
  local copies, waits for them, and re-layouts: 39 us -> 3.13 us
  between operations: 24.8 us -> 0.64 us
    psum x9 -> x0, blocking collectives: 354 us -> none  [the longest x8 313 us: local(): lax.psum((local_dots, jnp.sum(image * image)), ('grp', 'row'))]
    reduce_scatter x8 -> x0, waiting for transfers between devices: 264 us -> none  [local(): lax.psum_scatter(partial_image, 'row', scatter_dimension=1, tiled=True)]
    pallas_call x0 -> x1, Pallas kernels: none -> 148 us  [local(): pl.pallas_call(functools.partial(kernel, ngrp, nrow), out_shape=(jax.Shap...]
    dot_general x26 -> x0, matrix products: 73.3 us -> none  [the longest x8 70.8 us: local(): jnp.einsum('swba,swbc->sac', left_env, inner_terms, preferred_element_typ...]
    all_gather x1 -> x0, waiting for transfers between devices: 47.6 us -> none  [local(): right_full = lax.all_gather(right_env, 'row', axis=2, tiled=True)]
    div x7 -> x0, other arithmetic: 34 us -> none  [local(): krylov_basis.append(image / beta_norm)]
    reduce_sum x15 -> x0, other arithmetic: 24.4 us -> none  [the longest x8 19.7 us: local(): local_dots = jnp.stack([jnp.sum(vector * image) for vector in krylov_basis])]
    another operation x18 -> x0, local copies, waits for them, and re-layouts: 20.8 us -> none  [the longest x4 16.5 us: local(): local_dots = jnp.stack([jnp.sum(vector * image) for vector in krylov_basis])]
  transfers between devices with their start and end apart: 9 -> 0, of which waited for: 9 -> 0; matrix products, arithmetic and copies ran while one was open for 3% -> 0% of each run, Pallas kernels for 0% -> 0%
where the time goes in v1:
time: 152 us; the launch traced here: 151 us
  Pallas kernels  148 us (97%)
  local copies, waits for them, and re-layouts  3.13 us (2%)
    pallas_call x1, Pallas kernels, local(): pl.pallas_call(functools.partial(kernel, ngrp, nrow), out_shape=(jax.Shap...  148 us
    unnamed x2, local copies, waits for them, and re-layouts  3.13 us

profile of v1, /device:TPU:1, one launch (start us, length us, event | category | flops | bytes accessed | tf_op | source)
XLA Modules:
  0.0 151.4 jit_solution(1434651446200865988)
XLA Ops:
  0.6 147.6 %shard_map.59 = (f32[2,128,512]{2,1,0:T(8,128)}, f32[8,8]{1,0:T(8,128)}) custom-call(s32[2,2]{1,0:T(2,128)} %lengths.1, f32[2,128,512]{2,1,0:T(8,128)} %theta.1, bf16[2,8,128,512]{3,2,1,0:T(8,128)(2,1)} %left.1, bf16[2,8,128,512]{3,2,1,0:T(8,128)(2,1)} %right.1), custom_call_target="tpu_custom_call" | custom-call | tf_op jit(solution)/shard_map/pallas_call | solution.py:322
  148.2 1.9 %copy.8 = f32[2,128,512]{2,1,0:T(8,128)} copy(f32[2,128,512]{2,1,0:T(8,128)} %get-tuple-element.4) | data formatting | bytes 1048576
  150.1 1.3 copy.9

commit v2 on v1

--- a/solution.py
+++ b/solution.py
@@ -9,7 +9,7 @@
 
 KRYLOV = 8
 DEGREES = 19
-ROWS = 64
+ROWS = 32
 
 epsilon = 1e-06
 time_step = 0.5
@@ -19,7 +19,7 @@
 
 
 def kernel(ngrp, nrow, lengths, theta, left, right, out, hess,
-           masked, meta, l_land, l_t, r_land, q, basis, v, acc, live, msg, slots, h_t, evolved,
+           masked, meta, l_land, l_t, r_land, q, basis, img, v, acc, live, msg, slots, h_t, evolved, landed,
            th_send, th_recv, meta_send, meta_recv, l_send, l_recv, f_send, f_recv,
            r_send, r_recv, v_send, v_recv, m_send, m_recv, o_send, o_recv):
     S, lr, width = theta.shape
@@ -60,6 +60,7 @@
         square = square + jnp.sum((block * block).reshape(lr // 8, 8, width), axis=0)
     for k in range(1, K):
         basis[k] = jnp.zeros((width, half), F32)
+        img[k] = jnp.zeros((width, half), F32)
     h_t[...] = jnp.zeros_like(h_t)
 
     pl.semaphore_wait(barrier, n - 1)
@@ -119,16 +120,22 @@
             put(theta_piece(s, c), basis.at[0, my_rows, :], th_send.at[s, j, c], th_recv.at[r],
                 (base + c, t), (t == r) & (p == c))
 
-    def env(w, carry):
+    def send_left(w, carry):
+        for s, j, t in targets:
+            put(left.at[s, w], l_land.at[w, my_rows, :], l_send.at[w, s, j], l_recv.at[w, r],
+                (base + w % 2, t), (t == r) & (p == w % 2))
+        return carry
+
+    def send_right(w, carry):
         for s, j, t in targets:
             for c in range(2):
                 put(right.at[s, w, :, pl.ds(c * half, half)], r_land.at[w, my_rows, :],
                     r_send.at[w, s, j, c], r_recv.at[w, r], (base + c, t), (t == r) & (p == c))
-            put(left.at[s, w], l_land.at[w, my_rows, :], l_send.at[w, s, j], l_recv.at[w, r],
-                (base + w % 2, t), (t == r) & (p == w % 2))
-        return carry
-
-    lax.fori_loop(0, W, env, 0)
+        return carry
+
+    lax.fori_loop(0, 2, send_left, 0)
+    lax.fori_loop(0, W - 2, lambda w, c: send_right(w, send_left(w + 2, c)), 0)
+    lax.fori_loop(W - 2, W, send_right, 0)
 
     pltpu.make_async_copy(meta.at[1 - p], meta.at[1 - p], meta_recv).wait()
     a_len = meta[owner, pl.ds(2 * sector, 1), :]
@@ -164,85 +171,97 @@
         return pltpu.make_async_remote_copy(src_ref=l_land.at[w], dst_ref=l_land.at[w], send_sem=f_send.at[w],
                                             recv_sem=f_recv.at[w], device_id=partner, device_id_type=MESH)
 
+    acc[...] = jnp.zeros((width, half), F32)
+
+    def turn(w):
+        at = pl.ds(pl.multiple_of(w * width, width), width)
+        l_t[:, at] = l_land[w].T
+
     def image_zero(pair, carry):
-        mine = 2 * pair + p
+        mine, theirs = 2 * pair + p, 2 * pair + 1 - p
         for i in range(nrow):
             got(l_land.at[mine, pl.ds(i * lr, lr), :], l_recv.at[mine, i])
         forward_copy(mine).start()
+        turn(mine)
+        got(l_land.at[theirs], f_recv.at[theirs])
+        turn(theirs)
         for step in range(2):
             w = 2 * pair + step
             for i in range(nrow):
                 got(r_land.at[w, pl.ds(i * lr, lr), :], r_recv.at[w, i])
             at = pl.ds(pl.multiple_of(w * width, width), width)
             q[at, :] = jnp.dot(v[0], r_land[w], preferred_element_type=F32).astype(BF16)
-        theirs = 2 * pair + 1 - p
-        got(l_land.at[theirs], f_recv.at[theirs])
-        for step in range(2):
-            w = 2 * pair + step
-            at = pl.ds(pl.multiple_of(w * width, width), width)
-            l_t[:, at] = l_land[w].T
+        at = pl.ds(pl.multiple_of(pair * 2 * width, 2 * width), 2 * width)
+        acc[...] += jnp.dot(l_t[:, at], q[at, :], preferred_element_type=F32)
         return carry
 
     lax.fori_loop(0, W // 2, image_zero, 0)
 
-    def outer():
-        acc[...] = jnp.dot(l_t[...], q[...], preferred_element_type=F32)
-
-    outer()
-
     counts = jnp.where(r % rep == 0, 1.0, 0.0)
 
-    def coefficients(j):
+    def sweep(j, update, shift):
         def chunk(i, sums):
             rows = pl.ds(pl.multiple_of(i * ROWS, ROWS), ROWS)
-            u = acc[rows, :] * live[rows, :]
-            acc[rows, :] = u
-            new = []
-            for k in range(K + 1):
-                other = basis[k, rows, :] if k < K else u
-                new.append(sums[k] + jnp.sum((other * u).reshape(ROWS // 8, 8, half), axis=0))
+            b, u = update(rows)
+            new = [sums[k] + jnp.sum((basis[k, rows, :] * u).reshape(ROWS // 8, 8, half), axis=0) for k in range(K)]
+            new.append(sums[K] + jnp.sum((u * u).reshape(ROWS // 8, 8, half), axis=0))
+            v[j + 1, rows, my_cols] = (u - shift * b).astype(BF16)
             return tuple(new)
 
         zero = jnp.zeros((8, half), F32)
         sums = lax.fori_loop(0, width // ROWS, chunk, (zero,) * (K + 1))
+
+        @pl.when(j + 1 < K)
+        def _():
+            v_copy(j + 1).start()
+
         row = jnp.zeros((1, 128), F32)
         for k in range(K + 1):
             row = jnp.where(lane == k, jnp.sum(sums[k]), row)
         share(j, row * counts)
-        return shared(j)
-
-    def step(j, carry):
-        row = coefficients(j)
+
+    def first_update(rows):
+        u = acc[rows, :] * live[rows, :]
+        img[0, rows, :] = u
+        return basis[0, rows, :], u
+
+    no_shift = jnp.zeros((1, 1), F32)
+    sweep(0, first_update, no_shift)
+
+    def step(j, shift):
+        copy = v_copy(j + 1)
+        copy.wait()
+        vec = v.at[j + 1]
+        for w in range(W):
+            q[w * width:(w + 1) * width, :] = jnp.dot(vec[...], r_land[w], preferred_element_type=F32).astype(BF16)
+        acc[...] = jnp.dot(l_t[...], q[...], preferred_element_type=F32)
+
+        row = shared(j)
         dots = jnp.where(lane < K, row, 0.0)
         left_over = pick(row, K) - jnp.sum(dots * dots, axis=1, keepdims=True)
         beta = jnp.sqrt(jnp.maximum(left_over, 0.0) + epsilon)
         h_t[pl.ds(j, 1), :] = jnp.where(lane == j + 1, beta, dots)
-        coef = [pick(row, k) for k in range(K)]
         scale = 1.0 / beta
-
-        def chunk(i, c):
-            rows = pl.ds(pl.multiple_of(i * ROWS, ROWS), ROWS)
-            u = acc[rows, :]
+        rest = jnp.where(lane == j, dots - shift, dots)
+        for_basis = [pick(dots, k) * scale for k in range(K)]
+        for_image = [pick(rest, k) * scale for k in range(K)]
+
+        def update(rows):
+            b = img[j, rows, :] * scale
+            u = acc[rows, :] * (live[rows, :] * scale)
             for k in range(K):
-                u = u - coef[k] * basis[k, rows, :]
-            u = u * scale
-            basis[j + 1, rows, :] = u
-            v[j + 1, rows, my_cols] = u.astype(BF16)
-            return c
-
-        lax.fori_loop(0, width // ROWS, chunk, 0)
-        copy = v_copy(j + 1)
-        copy.start()
-        copy.wait()
-        vec = v.at[j + 1]
-
-        for w in range(W):
-            q[w * width:(w + 1) * width, :] = jnp.dot(vec[...], r_land[w], preferred_element_type=F32).astype(BF16)
-        outer()
-        return carry
-
-    lax.fori_loop(0, K - 1, step, 0)
-    row = coefficients(K - 1)
+                b = b - for_basis[k] * basis[k, rows, :]
+                u = u - for_image[k] * img[k, rows, :]
+            basis[j + 1, rows, :] = b
+            img[j + 1, rows, :] = u
+            return b, u
+
+        shift = pick(dots, j)
+        sweep(j + 1, update, shift)
+        return shift
+
+    lax.fori_loop(0, K - 1, step, no_shift)
+    row = shared(K - 1)
     h_t[pl.ds(K - 1, 1), :] = jnp.where(lane < K, row, 0.0)
 
     ht = h_t[...]
@@ -270,7 +289,7 @@
         total = weights[0] * basis[0, rows, :]
         for k in range(1, K):
             total = total + weights[k] * basis[k, rows, :]
-        evolved[rows, :] = total
+        evolved[rows, :] = total.astype(BF16)
         return c
 
     lax.fori_loop(0, width // ROWS, sum_chunk, 0)
@@ -278,12 +297,13 @@
     for t in range(nrow):
         @pl.when(r % rep == t % rep)
         def _():
-            put(evolved.at[pl.ds(t * lr, lr), :], out.at[sector, :, my_cols], o_send.at[t],
+            put(evolved.at[pl.ds(t * lr, lr), :], landed.at[sector, :, my_cols], o_send.at[t],
                 o_recv.at[sector, p], (base + owner, t), (r == t) & (p == owner))
 
     for s in range(S):
         for c in range(2):
-            got(out.at[s, :, pl.ds(c * half, half)], o_recv.at[s, c])
+            got(landed.at[s, :, pl.ds(c * half, half)], o_recv.at[s, c])
+        out[s] = landed[s].astype(F32)
     for t in range(nrow):
         @pl.when(r % rep == t % rep)
         def _():
@@ -323,7 +343,7 @@
         functools.partial(kernel, ngrp, nrow),
         out_shape=(jax.ShapeDtypeStruct(theta.shape, F32), jax.ShapeDtypeStruct((K, K), F32)),
         in_specs=[pl.BlockSpec(memory_space=pltpu.SMEM), vmem, hbm, hbm],
-        out_specs=(hbm, vmem),
+        out_specs=(vmem, vmem),
         scratch_shapes=[
             pltpu.VMEM((S, lr, width), F32),
             pltpu.VMEM((2, 8 * ((2 * S + 7) // 8), 128), F32),
@@ -332,13 +352,15 @@
             pltpu.VMEM((W, width, half), BF16),
             pltpu.VMEM((W * width, half), BF16),
             pltpu.VMEM((K, width, half), F32),
-            pltpu.VMEM((K, width, width), BF16),
+            pltpu.VMEM((K, width, half), F32),
+            pltpu.VMEM((K + 1, width, width), BF16),
             pltpu.VMEM((width, half), F32),
             pltpu.VMEM((width, half), F32),
             pltpu.VMEM((K + 1, 1, 128), F32),
             pltpu.VMEM((K + 1, n, 1, 128), F32),
             pltpu.VMEM((K, 128), F32),
-            pltpu.VMEM((width, half), F32),
+            pltpu.VMEM((width, half), BF16),
+            pltpu.VMEM((S, lr, width), BF16),
             dma((S, rep, 2)), dma((nrow,)), dma, dma,
             dma((W, S, rep)), dma((W, nrow)), dma((W,)), dma((W,)),
             dma((W, S, rep, 2)), dma((W, nrow)), dma((K,)), dma((K,)),

time: 152 us -> 123 us (0.81)
  Pallas kernels: 148 us -> 119 us
    pallas_call x1, Pallas kernels: 148 us -> 119 us  [local(): pl.pallas_call(functools.partial(kernel, ngrp, nrow), out_shape=(jax.Shap...]
where the time goes in v2:
time: 123 us
  Pallas kernels  119 us (97%)
  local copies, waits for them, and re-layouts  3.13 us (3%)
    pallas_call x1, Pallas kernels, local(): pl.pallas_call(functools.partial(kernel, ngrp, nrow), out_shape=(jax.Shap...  119 us
    unnamed x2, local copies, waits for them, and re-layouts  3.13 us

profile of v2, /device:TPU:1, one launch (start us, length us, event | category | flops | bytes accessed | tf_op | source)
XLA Modules:
  0.0 122.9 jit_solution(16340735260032988453)
XLA Ops:
  0.6 119.1 %shard_map.59 = (f32[2,128,512]{2,1,0:T(8,128)}, f32[8,8]{1,0:T(8,128)}) custom-call(s32[2,2]{1,0:T(2,128)} %lengths.1, f32[2,128,512]{2,1,0:T(8,128)} %theta.1, bf16[2,8,128,512]{3,2,1,0:T(8,128)(2,1)} %left.1, bf16[2,8,128,512]{3,2,1,0:T(8,128)(2,1)} %right.1), custom_call_target="tpu_custom_call" | custom-call | tf_op jit(solution)/shard_map/pallas_call | solution.py:342
  119.8 1.9 %copy.8 = f32[2,128,512]{2,1,0:T(8,128)} copy(f32[2,128,512]{2,1,0:T(8,128)} %get-tuple-element.4) | data formatting | bytes 1048576
  121.6 1.3 %copy.9 = f32[8,8]{1,0:T(8,128)} copy(f32[8,8]{1,0:T(8,128)} %get-tuple-element.5) | data formatting | bytes 512

commit v3 on v2

--- a/solution.py
+++ b/solution.py
@@ -19,7 +19,7 @@
 
 
 def kernel(ngrp, nrow, lengths, theta, left, right, out, hess,
-           masked, meta, l_land, l_t, r_land, q, basis, img, v, acc, live, msg, slots, h_t, evolved, landed,
+           masked, packed, meta, l_land, l_t, r_land, q, basis, img, v, acc, live, msg, slots, h_t, evolved, landed,
            th_send, th_recv, meta_send, meta_recv, l_send, l_recv, f_send, f_recv,
            r_send, r_recv, v_send, v_recv, m_send, m_recv, o_send, o_recv):
     S, lr, width = theta.shape
@@ -113,12 +113,7 @@
     targets = [(s, j, (p * S + s) * rep + j) for s in range(S) for j in range(rep)]
 
     def theta_piece(s, c):
-        return masked.at[s, :, pl.ds(c * half, half)]
-
-    for s, j, t in targets:
-        for c in range(2):
-            put(theta_piece(s, c), basis.at[0, my_rows, :], th_send.at[s, j, c], th_recv.at[r],
-                (base + c, t), (t == r) & (p == c))
+        return packed.at[s, :, pl.ds(c * half, half)]
 
     def send_left(w, carry):
         for s, j, t in targets:
@@ -134,9 +129,6 @@
         return carry
 
     lax.fori_loop(0, 2, send_left, 0)
-    lax.fori_loop(0, W - 2, lambda w, c: send_right(w, send_left(w + 2, c)), 0)
-    lax.fori_loop(W - 2, W, send_right, 0)
-
     pltpu.make_async_copy(meta.at[1 - p], meta.at[1 - p], meta_recv).wait()
     a_len = meta[owner, pl.ds(2 * sector, 1), :]
     c_len = meta[owner, pl.ds(2 * sector + 1, 1), :]
@@ -146,25 +138,31 @@
     col_ids = (p * half + lax.broadcasted_iota(jnp.int32, (width, half), 1)).astype(F32)
     live[...] = jnp.where((row_ids < a_len) & (col_ids < c_len), 1.0, 0.0)
 
+    norm_zero = jnp.sqrt(pick(shared(K), 0) + epsilon)
+    for s in range(S):
+        packed[s] = (masked[s] / norm_zero).astype(BF16)
+    for s, j, t in targets:
+        for c in range(2):
+            put(theta_piece(s, c), v.at[0, my_rows, pl.ds(c * half, half)], th_send.at[s, j, c], th_recv.at[r],
+                (base + c, t), (t == r) & (p == c))
+    lax.fori_loop(0, W - 2, lambda w, c: send_right(w, send_left(w + 2, c)), 0)
+    lax.fori_loop(W - 2, W, send_right, 0)
+
     def v_copy(j):
         return pltpu.make_async_remote_copy(src_ref=v.at[j, :, my_cols], dst_ref=v.at[j, :, my_cols],
                                             send_sem=v_send.at[j], recv_sem=v_recv.at[j],
                                             device_id=partner, device_id_type=MESH)
 
-    norm_zero = jnp.sqrt(pick(shared(K), 0) + epsilon)
     for i in range(nrow):
-        got(basis.at[0, pl.ds(i * lr, lr), :], th_recv.at[i])
-
+        got(v.at[0, pl.ds(i * lr, lr), my_cols], th_recv.at[i])
+    first = v_copy(0)
+    first.start()
     def start_chunk(i, c):
         rows = pl.ds(pl.multiple_of(i * ROWS, ROWS), ROWS)
-        b = basis[0, rows, :] / norm_zero
-        basis[0, rows, :] = b
-        v[0, rows, my_cols] = b.astype(BF16)
+        basis[0, rows, :] = v[0, rows, my_cols].astype(F32)
         return c
 
     lax.fori_loop(0, width // ROWS, start_chunk, 0)
-    first = v_copy(0)
-    first.start()
     first.wait()
 
     def forward_copy(w):
@@ -199,25 +197,26 @@
 
     counts = jnp.where(r % rep == 0, 1.0, 0.0)
 
-    def sweep(j, update, shift):
+    def sweep(j, have, update, shift):
         def chunk(i, sums):
             rows = pl.ds(pl.multiple_of(i * ROWS, ROWS), ROWS)
             b, u = update(rows)
-            new = [sums[k] + jnp.sum((basis[k, rows, :] * u).reshape(ROWS // 8, 8, half), axis=0) for k in range(K)]
-            new.append(sums[K] + jnp.sum((u * u).reshape(ROWS // 8, 8, half), axis=0))
+            new = [sums[k] + jnp.sum((basis[k, rows, :] * u).reshape(ROWS // 8, 8, half), axis=0)
+                   for k in range(have)]
+            new.append(sums[have] + jnp.sum((u * u).reshape(ROWS // 8, 8, half), axis=0))
             v[j + 1, rows, my_cols] = (u - shift * b).astype(BF16)
             return tuple(new)
 
         zero = jnp.zeros((8, half), F32)
-        sums = lax.fori_loop(0, width // ROWS, chunk, (zero,) * (K + 1))
+        sums = lax.fori_loop(0, width // ROWS, chunk, (zero,) * (have + 1))
 
         @pl.when(j + 1 < K)
         def _():
             v_copy(j + 1).start()
 
         row = jnp.zeros((1, 128), F32)
-        for k in range(K + 1):
-            row = jnp.where(lane == k, jnp.sum(sums[k]), row)
+        for k in range(have + 1):
+            row = jnp.where(lane == (k if k < have else K), jnp.sum(sums[k]), row)
         share(j, row * counts)
 
     def first_update(rows):
@@ -226,9 +225,10 @@
         return basis[0, rows, :], u
 
     no_shift = jnp.zeros((1, 1), F32)
-    sweep(0, first_update, no_shift)
-
-    def step(j, shift):
+    sweep(0, 1, first_update, no_shift)
+
+    def step(have, j, carry):
+        shift, trace = carry
         copy = v_copy(j + 1)
         copy.wait()
         vec = v.at[j + 1]
@@ -243,13 +243,14 @@
         h_t[pl.ds(j, 1), :] = jnp.where(lane == j + 1, beta, dots)
         scale = 1.0 / beta
         rest = jnp.where(lane == j, dots - shift, dots)
-        for_basis = [pick(dots, k) * scale for k in range(K)]
-        for_image = [pick(rest, k) * scale for k in range(K)]
+        for_basis = [pick(dots, k) * scale for k in range(have - 1)]
+        for_image = [pick(rest, k) * scale for k in range(have - 1)]
+        trace = jnp.where(lane == j + 1, -scale * jnp.sum(dots * trace, axis=1, keepdims=True), trace)
 
         def update(rows):
             b = img[j, rows, :] * scale
             u = acc[rows, :] * (live[rows, :] * scale)
-            for k in range(K):
+            for k in range(have - 1):
                 b = b - for_basis[k] * basis[k, rows, :]
                 u = u - for_image[k] * img[k, rows, :]
             basis[j + 1, rows, :] = b
@@ -257,10 +258,14 @@
             return b, u
 
         shift = pick(dots, j)
-        sweep(j + 1, update, shift)
-        return shift
-
-    lax.fori_loop(0, K - 1, step, no_shift)
+        sweep(j + 1, have, update, shift)
+        return shift, trace
+
+    carry = (no_shift, jnp.where(lane == 0, 1.0, 0.0))
+    for start in range(0, K - 1, 2):
+        end = min(start + 2, K - 1)
+        carry = lax.fori_loop(start, end, functools.partial(step, end + 1), carry)
+    trace = carry[1]
     row = shared(K - 1)
     h_t[pl.ds(K - 1, 1), :] = jnp.where(lane < K, row, 0.0)
 
@@ -282,12 +287,14 @@
         else:
             term = jnp.sum((time_step * ht) * term, axis=0, keepdims=True) * (1.0 / degree)
             series_row = series_row + term
-    weights = [(pick(series_row, k) + series_col[k:k + 1, :]) * norm_zero for k in range(K)]
+    weights = [pick(series_row, k) + series_col[k:k + 1, :] for k in range(K)]
+    fix = sum(pick(trace, k) * weights[k] for k in range(1, K))
+    weights = weights[:1] + [weight * norm_zero for weight in weights[1:]]
 
     def sum_chunk(i, c):
         rows = pl.ds(pl.multiple_of(i * ROWS, ROWS), ROWS)
-        total = weights[0] * basis[0, rows, :]
-        for k in range(1, K):
+        total = weights[1] * basis[1, rows, :]
+        for k in range(2, K):
             total = total + weights[k] * basis[k, rows, :]
         evolved[rows, :] = total.astype(BF16)
         return c
@@ -303,7 +310,8 @@
     for s in range(S):
         for c in range(2):
             got(landed.at[s, :, pl.ds(c * half, half)], o_recv.at[s, c])
-        out[s] = landed[s].astype(F32)
+        out[s] = landed[s].astype(F32) + weights[0] * masked[s]
+        out[s] += fix * (masked[s] - norm_zero * packed[s].astype(F32))
     for t in range(nrow):
         @pl.when(r % rep == t % rep)
         def _():
@@ -346,6 +354,7 @@
         out_specs=(vmem, vmem),
         scratch_shapes=[
             pltpu.VMEM((S, lr, width), F32),
+            pltpu.VMEM((S, lr, width), BF16),
             pltpu.VMEM((2, 8 * ((2 * S + 7) // 8), 128), F32),
             pltpu.VMEM((W, width, width), BF16),
             pltpu.VMEM((width, W * width), BF16),

time: 123 us -> 117 us (0.951)
  Pallas kernels: 119 us -> 113 us
    pallas_call x1, Pallas kernels: 119 us -> 113 us  [local(): pl.pallas_call(functools.partial(kernel, ngrp, nrow), out_shape=(jax.Shap...]
where the time goes in v3:
time: 117 us
  Pallas kernels  113 us (97%)
  local copies, waits for them, and re-layouts  3.13 us (3%)
    pallas_call x1, Pallas kernels, local(): pl.pallas_call(functools.partial(kernel, ngrp, nrow), out_shape=(jax.Shap...  113 us
    unnamed x2, local copies, waits for them, and re-layouts  3.13 us

profile of v3, /device:TPU:1, one launch (start us, length us, event | category | flops | bytes accessed | tf_op | source)
XLA Modules:
  0.0 117.2 jit_solution(6547745473404798651)
XLA Ops:
  0.6 113.4 %shard_map.59 = (f32[2,128,512]{2,1,0:T(8,128)}, f32[8,8]{1,0:T(8,128)}) custom-call(s32[2,2]{1,0:T(2,128)} %lengths.1, f32[2,128,512]{2,1,0:T(8,128)} %theta.1, bf16[2,8,128,512]{3,2,1,0:T(8,128)(2,1)} %left.1, bf16[2,8,128,512]{3,2,1,0:T(8,128)(2,1)} %right.1), custom_call_target="tpu_custom_call" | custom-call | tf_op jit(solution)/shard_map/pallas_call | solution.py:350
  114.0 1.9 %copy.8 = f32[2,128,512]{2,1,0:T(8,128)} copy(f32[2,128,512]{2,1,0:T(8,128)} %get-tuple-element.4) | data formatting | bytes 1048576
  115.9 1.3 %copy.9 = f32[8,8]{1,0:T(8,128)} copy(f32[8,8]{1,0:T(8,128)} %get-tuple-element.5) | data formatting | bytes 512

commit v4 on v3

--- a/solution.py
+++ b/solution.py
@@ -18,8 +18,8 @@
 BF16 = jnp.bfloat16
 
 
-def kernel(ngrp, nrow, lengths, theta, left, right, out, hess,
-           masked, packed, meta, l_land, l_t, r_land, q, basis, img, v, acc, live, msg, slots, h_t, evolved, landed,
+def kernel(ngrp, nrow, lengths, theta, left, right, landed, small,
+           masked, packed, meta, l_land, l_t, r_land, q, basis, img, v, acc, live, msg, slots, h_t, evolved,
            th_send, th_recv, meta_send, meta_recv, l_send, l_recv, f_send, f_recv,
            r_send, r_recv, v_send, v_recv, m_send, m_recv, o_send, o_recv):
     S, lr, width = theta.shape
@@ -87,14 +87,20 @@
         msg[k] = row
         slots[k, me] = row
 
-        def one(o, c):
-            t = (me + o) % n
+        def send(tg, tr):
             pltpu.make_async_remote_copy(src_ref=msg.at[k], dst_ref=slots.at[k, me], send_sem=m_send.at[k],
-                                         recv_sem=m_recv.at[k], device_id=(t // nrow, t % nrow),
-                                         device_id_type=MESH).start()
+                                         recv_sem=m_recv.at[k], device_id=(tg, tr), device_id_type=MESH).start()
+
+        def group(o, c):
+            tg = (g + ngrp // 2 + o) % ngrp
+            for d in range(nrow):
+                send(tg, (r + d) % nrow)
             return c
 
-        lax.fori_loop(1, n, one, 0)
+        lax.fori_loop(0, ngrp - ngrp // 2, group, 0)
+        lax.fori_loop(ngrp - ngrp // 2 + 1, ngrp, group, 0)
+        for d in range(1, nrow):
+            send(g, (r + d) % nrow)
 
     def shared(k):
         rest = slots.at[k, pl.ds(0, n - 1)]
@@ -276,7 +282,6 @@
     for j in range(K):
         column = jnp.sum(jnp.where(lanes == sub, ht[j:j + 1, :], 0.0), axis=1, keepdims=True)
         h = jnp.where(lanes == j, column, h)
-    hess[...] = h[:, :K]
     term = jnp.where(lane == 0, 1.0, 0.0)
     series_row = term
     series_col = jnp.zeros((K, 1), F32)
@@ -289,6 +294,8 @@
             series_row = series_row + term
     weights = [pick(series_row, k) + series_col[k:k + 1, :] for k in range(K)]
     fix = sum(pick(trace, k) * weights[k] for k in range(1, K))
+    small[0:K, :] = h
+    small[K:K + 1, :] = jnp.where(lane == 0, weights[0], jnp.where(lane == 1, fix, norm_zero))
     weights = weights[:1] + [weight * norm_zero for weight in weights[1:]]
 
     def sum_chunk(i, c):
@@ -310,8 +317,6 @@
     for s in range(S):
         for c in range(2):
             got(landed.at[s, :, pl.ds(c * half, half)], o_recv.at[s, c])
-        out[s] = landed[s].astype(F32) + weights[0] * masked[s]
-        out[s] += fix * (masked[s] - norm_zero * packed[s].astype(F32))
     for t in range(nrow):
         @pl.when(r % rep == t % rep)
         def _():
@@ -335,6 +340,19 @@
         return carry
 
     lax.fori_loop(0, W // 2, forward_done, 0)
+
+
+def combine(lengths, theta, landed, small, out, hess):
+    S, lr, width = theta.shape
+    K = KRYLOV
+    weight, fix, norm_zero = small[K:K + 1, 0:1], small[K:K + 1, 1:2], small[K:K + 1, 2:3]
+    row_ids = lax.axis_index("row") * lr + lax.broadcasted_iota(jnp.int32, (lr, width), 0)
+    col_ids = lax.broadcasted_iota(jnp.int32, (lr, width), 1)
+    for s in range(S):
+        masked = jnp.where((row_ids < lengths[s, 0]) & (col_ids < lengths[s, 1]), theta[s], 0.0)
+        rounded = (masked / norm_zero).astype(BF16).astype(F32)
+        out[s] = landed[s].astype(F32) + weight * masked + fix * (masked - norm_zero * rounded)
+    hess[...] = small[:K, :K]
 
 
 def local(ngrp, nrow, theta, left_env, right_env, lengths):
@@ -347,11 +365,11 @@
     dma = pltpu.SemaphoreType.DMA
     vmem = pl.BlockSpec(memory_space=pltpu.VMEM)
     hbm = pl.BlockSpec(memory_space=pl.ANY)
-    return pl.pallas_call(
+    landed, small = pl.pallas_call(
         functools.partial(kernel, ngrp, nrow),
-        out_shape=(jax.ShapeDtypeStruct(theta.shape, F32), jax.ShapeDtypeStruct((K, K), F32)),
+        out_shape=(jax.ShapeDtypeStruct(theta.shape, BF16), jax.ShapeDtypeStruct((K + 8, 128), F32)),
         in_specs=[pl.BlockSpec(memory_space=pltpu.SMEM), vmem, hbm, hbm],
-        out_specs=(vmem, vmem),
+        out_specs=(hbm, vmem),
         scratch_shapes=[
             pltpu.VMEM((S, lr, width), F32),
             pltpu.VMEM((S, lr, width), BF16),
@@ -369,7 +387,6 @@
             pltpu.VMEM((K + 1, n, 1, 128), F32),
             pltpu.VMEM((K, 128), F32),
             pltpu.VMEM((width, half), BF16),
-            pltpu.VMEM((S, lr, width), BF16),
             dma((S, rep, 2)), dma((nrow,)), dma, dma,
             dma((W, S, rep)), dma((W, nrow)), dma((W,)), dma((W,)),
             dma((W, S, rep, 2)), dma((W, nrow)), dma((K,)), dma((K,)),
@@ -378,6 +395,12 @@
         compiler_params=pltpu.CompilerParams(collective_id=0, has_side_effects=True,
                                              vmem_limit_bytes=60 * 1024 * 1024),
     )(lengths, theta, left_env, right_env)
+    return pl.pallas_call(
+        combine,
+        out_shape=(jax.ShapeDtypeStruct(theta.shape, F32), jax.ShapeDtypeStruct((K, K), F32)),
+        in_specs=[pl.BlockSpec(memory_space=pltpu.SMEM), vmem, vmem, vmem],
+        out_specs=(vmem, vmem),
+    )(lengths, theta, landed, small)
 
 
 def solution(mesh):

time: 117 us -> 114 us (0.974)
  local copies, waits for them, and re-layouts: 3.13 us -> 0 us
    unnamed x2 -> x0, local copies, waits for them, and re-layouts: 3.13 us -> none
    pallas_call x1, Pallas kernels: 113 us -> 111 us  [local(): pl.pallas_call(functools.partial(kernel, ngrp, nrow), out_shape=(jax.Shap...]
    pallas_call x0 -> x1, Pallas kernels: none -> 2.28 us  [local(): pl.pallas_call(combine, out_shape=(jax.ShapeDtypeStruct(theta.shape, F32)...]
where the time goes in v4:
time: 114 us
  Pallas kernels  113 us (99%)
    pallas_call x1, Pallas kernels, local(): pl.pallas_call(functools.partial(kernel, ngrp, nrow), out_shape=(jax.Shap...  111 us
    pallas_call x1, Pallas kernels, local(): pl.pallas_call(combine, out_shape=(jax.ShapeDtypeStruct(theta.shape, F32)...  2.28 us

profile of v4, /device:TPU:1, one launch (start us, length us, event | category | flops | bytes accessed | tf_op | source)
XLA Modules:
  0.0 114.0 jit_solution(15488832430014668983)
XLA Ops:
  0.6 111.0 %shard_map.59 = (bf16[2,128,512]{2,1,0:T(8,128)(2,1)}, f32[16,128]{1,0:T(8,128)}) custom-call(s32[2,2]{1,0:T(2,128)} %lengths.3, f32[2,128,512]{2,1,0:T(8,128)} %theta.3, bf16[2,8,128,512]{3,2,1,0:T(8,128)(2,1)} %left.1, bf16[2,8,128,512]{3,2,1,0:T(8,128)(2,1)} %right.1), custom_call_target="tpu_custom_call" | custom-call | tf_op jit(solution)/shard_map/pallas_call | solution.py:368
  111.7 2.3 %shard_map.60 = (f32[2,128,512]{2,1,0:T(8,128)}, f32[8,8]{1,0:T(8,128)}) custom-call(s32[2,2]{1,0:T(2,128)} %lengths.3, f32[2,128,512]{2,1,0:T(8,128)} %theta.3, bf16[2,128,512]{2,1,0:T(8,128)(2,1)} %get-tuple-element.4.landed, f32[16,128]{1,0:T(8,128)} %get-tuple-element.5.small), custom_call_target="tpu_custom_call" | custom-call | tf_op jit(solution)/shard_map/pallas_call | solution.py:398
